TPU v7x, 32 devices: a whole 2x2x4 slice. The times are simulated.
32 devices in a mesh: ids: 8 (over z, x), mdl: 4 (over y, core).
Axes of the slice: x: 2, y: 2, z: 4, core: 2. Of those that a mesh axis runs over, the one named last changes fastest.
Arguments:
- hash_codes: int32 [32768, 1024], P('ids', 'mdl'), may hold values from 0 to 1023
- request_ids: int32 [64, 1024], P('ids'), may hold values from 0 to 32767, as said below
- request_counts: int32 [64], P('ids'), may hold values from 256 to 1024, as said below
- token_slots: int32 [65536], P('ids'), may hold values from 0 to 8191, as said below
- cotangent: bfloat16 [65536, 32], P('ids'), may hold values from -6 to 6
- weight_first: float32 [1024, 1800], P('ids', 'mdl'), may hold values from -0.1875 to 0.1875
- weight_second: float32 [1800, 1800], P(None, 'mdl'), may hold values from -0.125 to 0.125
- weight_final: float32 [1800, 32], P('mdl'), may hold values from -0.125 to 0.125
- norm_params: float32 [4, 1800], P(None, 'mdl')
- bias_final: float32 [32], replicated, may hold values from -0.5 to 0.5
- moment_first: float32 [1024, 1800], P('ids', 'mdl'), may hold values from -0.0007324219 to 0.0007324219
- square_first: float32 [1024, 1800], P('ids', 'mdl'), may hold values from 1.373291e-09 to 5.493164e-09
- moment_second: float32 [1800, 1800], P(None, 'mdl'), may hold values from -0.0007324219 to 0.0007324219
- square_second: float32 [1800, 1800], P(None, 'mdl'), may hold values from 1.373291e-09 to 5.493164e-09
- moment_final: float32 [1800, 32], P('mdl'), may hold values from -0.0048828125 to 0.0048828125
- square_final: float32 [1800, 32], P('mdl'), may hold values from 6.103516e-08 to 2.4414064e-07
- moment_norm: float32 [4, 1800], P(None, 'mdl'), may hold values from -0.001953125 to 0.001953125
- square_norm: float32 [4, 1800], P(None, 'mdl'), may hold values from 9e-09 to 3.6e-08
- moment_bias: float32 [32], replicated, may hold values from -0.03125 to 0.03125
- square_bias: float32 [32], replicated, may hold values from 2.5e-06 to 1e-05
Outputs:
- token_embed: bfloat16 [65536, 32], P('ids')
- momentum_first: float32 [1024, 1800], P('ids', 'mdl')
- variance_first: float32 [1024, 1800], P('ids', 'mdl')
- master_first: float32 [1024, 1800], P('ids', 'mdl')
- bfloat_first: bfloat16 [1024, 1800], P('ids', 'mdl')
- momentum_second: float32 [1800, 1800], P(None, 'mdl')
- variance_second: float32 [1800, 1800], P(None, 'mdl')
- master_second: float32 [1800, 1800], P(None, 'mdl')
- bfloat_second: bfloat16 [1800, 1800], P(None, 'mdl')
- momentum_final: float32 [1800, 32], P('mdl')
- variance_final: float32 [1800, 32], P('mdl')
- master_final: float32 [1800, 32], P('mdl')
- bfloat_final: bfloat16 [1800, 32], P('mdl')
- momentum_norm: float32 [4, 1800], P(None, 'mdl')
- variance_norm: float32 [4, 1800], P(None, 'mdl')
- master_norm: float32 [4, 1800], P(None, 'mdl')
- momentum_bias: float32 [32], replicated
- variance_bias: float32 [32], replicated
- master_bias: float32 [32], replicated
Inputs may be any that keep to these rules, and one draw needn't show every extreme that they name: `request_ids`: entries of row s * 8 + j lie in owner j's range j * 4096 to (j + 1) * 4096 - 1; the live ones (the first request_counts of the row) are distinct; the others are padding. `request_counts`: some owner receives exactly 1024 live ids from every device. `token_slots`: each token points at a live slot of its own device, and every live slot of a device is pointed at by one or more of its tokens.
All inputs are finite; a program needn't handle non-finite values.
Results may differ from a plain program's by a relative error of at most 0.003.
The roundings to bfloat16 on the way count: a program that leaves them out, or rounds other values in their place, can miss the bound.
Values may be sent and summed in bfloat16 or wider, within the bound.
A program may use at most 256 MiB of HBM per device.

v0:
```python
import jax
import jax.numpy as jnp
from jax import lax
from jax.sharding import PartitionSpec as P

STEP = 10
beta_one = 0.9
beta_two = 0.999
adam_epsilon = 1e-08
norm_epsilon = 1e-05
penalty_weight = 0.25
decay_matrix = 0.01
rate_matrix = 0.05
rate_norm = 0.5
rate_bias = 0.02
LANES = 128


def mish_parts(inputs):
    grown = jnp.exp(jnp.minimum(inputs, 20.0))
    above = grown * (grown + 2.0)
    inverse = 1.0 / (above + 2.0)
    return (grown, above * inverse, inverse)


def mish(inputs):
    return inputs * mish_parts(inputs)[1]


def mish_slope(inputs):
    grown, gate, inverse = mish_parts(inputs)
    return gate + 4.0 * jnp.minimum(inputs, 20.0) * (grown * inverse) * ((1.0 + grown) * inverse)


def contract(left, right, left_dim, right_dim):
    return lax.dot_general(
        left, right, (((left_dim,), (right_dim,)), ((), ())), preferred_element_type=jnp.float32
    )


def norm_back(upstream, unit_rows, gain_row, scale_row, live_mask, gain_sum, shift_sum, live_count):
    return scale_row * (
        gain_row * upstream
        - live_mask[:, None] * gain_row * (shift_sum + unit_rows * gain_sum) / live_count
    )


def adam(weight, moment, square, gradient, step_rate, shrink):
    momentum = beta_one * moment + (1.0 - beta_one) * gradient
    variance = beta_two * square + (1.0 - beta_two) * gradient * gradient
    moment_hat = momentum / (1.0 - beta_one**STEP)
    square_hat = variance / (1.0 - beta_two**STEP)
    master = weight - step_rate * (
        moment_hat / (jnp.sqrt(square_hat) + adam_epsilon) + shrink * weight
    )
    return (momentum, variance, master)


def split_two(values):
    high = values.astype(jnp.bfloat16)
    low = (values - high.astype(jnp.float32)).astype(jnp.bfloat16)
    return (high, low)


def one_hot(index, length, first):
    rows = lax.broadcasted_iota(jnp.int32, (length, index.shape[0]), 0) + first
    return (rows == index[None, :]).astype(jnp.bfloat16)


def body(
    hash_codes,
    request_ids,
    request_counts,
    token_slots,
    cotangent,
    weight_first,
    weight_second,
    weight_final,
    norm_params,
    bias_final,
    moment_first,
    square_first,
    moment_second,
    square_second,
    moment_final,
    square_final,
    moment_norm,
    square_norm,
    moment_bias,
    square_bias,
):
    owners = lax.axis_size("ids")
    parts = lax.axis_size("mdl")
    part = lax.axis_index("mdl")
    both = ("ids", "mdl")
    range_rows = hash_codes.shape[0]
    rows = range_rows // parts
    slots_per = request_ids.shape[1]
    piece = slots_per // parts
    out_width = weight_final.shape[1]
    width = weight_first.shape[1]
    wide = width + -width % LANES
    hidden = wide * parts
    more = wide - width
    token_count = token_slots.shape[0]
    token_piece = token_count // parts
    token_total = token_count * owners
    first_part = jnp.pad(weight_first.astype(jnp.bfloat16), ((0, 0), (0, more)))
    first_low = lax.all_gather(first_part, "ids", axis=0, tiled=True)
    first_low = lax.all_gather(first_low, "mdl", axis=1, tiled=True)
    second_part = jnp.pad(
        weight_second.astype(jnp.bfloat16).reshape(parts, width, width),
        ((0, 0), (0, more), (0, more)),
    ).reshape(hidden, wide)
    second_low = lax.all_gather(second_part, "mdl", axis=1, tiled=True)
    final_part = jnp.pad(weight_final.astype(jnp.bfloat16), ((0, more), (0, 0)))
    final_low = lax.all_gather(final_part, "mdl", axis=0, tiled=True)
    norm_all = lax.all_gather(jnp.pad(norm_params, ((0, 0), (0, more))), "mdl", axis=1, tiled=True)
    encoded = ((hash_codes.astype(jnp.float32) + 0.5) / 512.0 - 1.0).astype(jnp.bfloat16)
    features = lax.all_to_all(encoded, "mdl", split_axis=0, concat_axis=1, tiled=True)
    owner_row = jnp.arange(owners, dtype=jnp.int32)[:, None]
    wanted = jnp.where(
        jnp.arange(slots_per, dtype=jnp.int32)[None, :] < request_counts[:, None],
        request_ids - owner_row * range_rows,
        range_rows,
    )
    received = lax.all_to_all(wanted, "ids", split_axis=0, concat_axis=0, tiled=True)
    slot_owner = token_slots // slots_per
    slot_place = token_slots % slots_per - part * piece
    slot_here = jnp.where(
        (slot_place >= 0) & (slot_place < piece), slot_owner * piece + slot_place, -1
    )
    slot_sum = (
        jnp.dot(
            one_hot(slot_here, owners * piece, 0), cotangent, preferred_element_type=jnp.float32
        )
        / token_total
    )
    high, low = split_two(slot_sum)
    sent = jnp.concatenate([high, low], axis=1).reshape(owners, piece * 2 * out_width)
    arrived = lax.all_to_all(sent, "ids", split_axis=0, concat_axis=0, tiled=True)
    arrived = lax.all_gather(
        arrived.reshape(owners * piece, 2 * out_width), "mdl", axis=0, tiled=False
    )
    arrived = arrived.reshape(parts * owners * piece, 2 * out_width)
    slot_rows = received.reshape(owners, parts, piece).transpose(1, 0, 2)
    slot_rows = slot_rows.reshape(-1)
    marked = jnp.concatenate(
        [arrived, jnp.ones((arrived.shape[0], 2 * out_width), jnp.bfloat16)], axis=1
    )
    row_sums = jnp.dot(
        one_hot(slot_rows, rows, part * rows), marked, preferred_element_type=jnp.float32
    )
    row_grad = row_sums[:, :out_width] + row_sums[:, out_width : 2 * out_width]
    live_mask = jnp.minimum(row_sums[:, 2 * out_width], 1.0)
    linear_one = jnp.dot(features, first_low, preferred_element_type=jnp.float32)
    active_one = mish(linear_one)
    weighted_one = live_mask[:, None] * active_one
    sums_one = jnp.stack([jnp.sum(weighted_one, 0), jnp.sum(weighted_one * active_one, 0)])
    sums_one, live_count = lax.psum((sums_one, jnp.sum(live_mask)), both)
    mean_one = sums_one[0] / live_count
    scale_one = lax.rsqrt(sums_one[1] / live_count - mean_one * mean_one + norm_epsilon)
    unit_one = (active_one - mean_one) * scale_one
    normed_one = (norm_all[0] * unit_one + norm_all[1]).astype(jnp.bfloat16)
    linear_two = jnp.dot(normed_one, second_low, preferred_element_type=jnp.float32)
    active_two = mish(linear_two)
    weighted_two = live_mask[:, None] * active_two
    sums_two = lax.psum(
        jnp.stack([jnp.sum(weighted_two, 0), jnp.sum(weighted_two * active_two, 0)]), both
    )
    mean_two = sums_two[0] / live_count
    scale_two = lax.rsqrt(sums_two[1] / live_count - mean_two * mean_two + norm_epsilon)
    unit_two = (active_two - mean_two) * scale_two
    normed_two = (norm_all[2] * unit_two + norm_all[3]).astype(jnp.bfloat16)
    embedding = jnp.dot(normed_two, final_low, preferred_element_type=jnp.float32) + bias_final
    embed_low = embedding.astype(jnp.bfloat16)
    embed_range = lax.all_gather(embed_low, "mdl", axis=0, tiled=True)
    slots_mine = lax.dynamic_slice(received, (0, part * piece), (owners, piece)).reshape(-1)
    pick_rows = (
        slots_mine[:, None] == lax.broadcasted_iota(jnp.int32, (owners * piece, range_rows), 1)
    ).astype(jnp.bfloat16)
    replies = jnp.dot(pick_rows, embed_range, preferred_element_type=jnp.float32)
    replies = replies.astype(jnp.bfloat16).reshape(owners, piece * out_width)
    returned = lax.all_to_all(replies, "ids", split_axis=0, concat_axis=0, tiled=True)
    returned = lax.all_gather(returned.reshape(owners, piece, out_width), "mdl", axis=1, tiled=True)
    returned = returned.reshape(owners * slots_per, out_width)
    tokens_mine = lax.dynamic_slice(token_slots, (part * token_piece,), (token_piece,))
    pick_slots = (
        tokens_mine[:, None]
        == lax.broadcasted_iota(jnp.int32, (token_piece, owners * slots_per), 1)
    ).astype(jnp.bfloat16)
    token_part = jnp.dot(pick_slots, returned, preferred_element_type=jnp.float32)
    token_embed = lax.all_gather(token_part.astype(jnp.bfloat16), "mdl", axis=0, tiled=True)
    grad_embed = (
        row_grad + 2.0 * penalty_weight / live_count * live_mask[:, None] * embedding
    ).astype(jnp.bfloat16)
    incoming_two = contract(grad_embed, final_low, 1, 1)
    sums_two = lax.psum(
        jnp.stack([jnp.sum(incoming_two * unit_two, 0), jnp.sum(incoming_two, 0)]), both
    )
    local_final = contract(normed_two, grad_embed, 0, 0)
    local_bias = jnp.sum(grad_embed.astype(jnp.float32), 0)
    outgoing_two = norm_back(
        incoming_two,
        unit_two,
        norm_all[2],
        scale_two,
        live_mask,
        sums_two[0],
        sums_two[1],
        live_count,
    )
    grad_linear_two = (mish_slope(linear_two) * outgoing_two).astype(jnp.bfloat16)
    local_second = jnp.stack(
        [
            contract(normed_one, grad_linear_two[:, wide * k : wide * (k + 1)], 0, 0)
            for k in range(parts)
        ]
    )
    grad_second = lax.psum_scatter(local_second, "mdl", scatter_dimension=0, tiled=False)
    grad_second = lax.psum(grad_second, "ids")
    grad_second = grad_second.reshape(parts, wide, wide)[:, :width, :width].reshape(-1, width)
    incoming_one = contract(grad_linear_two, second_low, 1, 1)
    sums_one, final_sum, grad_bias = lax.psum(
        (
            jnp.stack([jnp.sum(incoming_one * unit_one, 0), jnp.sum(incoming_one, 0)]),
            local_final,
            local_bias,
        ),
        both,
    )
    outgoing_one = norm_back(
        incoming_one,
        unit_one,
        norm_all[0],
        scale_one,
        live_mask,
        sums_one[0],
        sums_one[1],
        live_count,
    )
    grad_linear_one = (mish_slope(linear_one) * outgoing_one).astype(jnp.bfloat16)
    local_first = jnp.stack(
        [
            contract(features, grad_linear_one[:, wide * k : wide * (k + 1)], 0, 0)
            for k in range(parts)
        ]
    )
    grad_first = lax.psum_scatter(local_first, "mdl", scatter_dimension=0, tiled=False)
    grad_first = lax.psum_scatter(grad_first, "ids", scatter_dimension=0, tiled=True)[:, :width]
    start = part * wide
    grad_final = lax.dynamic_slice(final_sum, (start, 0), (width, out_width))
    grad_norm = lax.dynamic_slice(jnp.concatenate([sums_one, sums_two]), (0, start), (4, width))
    momentum_first, variance_first, master_first = adam(
        weight_first, moment_first, square_first, grad_first, rate_matrix, decay_matrix
    )
    momentum_second, variance_second, master_second = adam(
        weight_second, moment_second, square_second, grad_second, rate_matrix, decay_matrix
    )
    momentum_final, variance_final, master_final = adam(
        weight_final, moment_final, square_final, grad_final, rate_matrix, decay_matrix
    )
    momentum_norm, variance_norm, master_norm = adam(
        norm_params, moment_norm, square_norm, grad_norm, rate_norm, 0.0
    )
    momentum_bias, variance_bias, master_bias = adam(
        bias_final, moment_bias, square_bias, grad_bias, rate_bias, 0.0
    )
    return (
        token_embed,
        momentum_first,
        variance_first,
        master_first,
        master_first.astype(jnp.bfloat16),
        momentum_second,
        variance_second,
        master_second,
        master_second.astype(jnp.bfloat16),
        momentum_final,
        variance_final,
        master_final,
        master_final.astype(jnp.bfloat16),
        momentum_norm,
        variance_norm,
        master_norm,
        momentum_bias,
        variance_bias,
        master_bias,
    )


def solution(mesh):
    rows = P("ids", None)
    grid = P("ids", "mdl")
    columns = P(None, "mdl")
    mdl_rows = P("mdl", None)
    return jax.shard_map(
        body,
        mesh=mesh,
        in_specs=(grid, rows, P("ids"), P("ids"), rows, grid, columns, mdl_rows, columns, P())
        + (grid,) * 2
        + (columns,) * 2
        + (mdl_rows,) * 2
        + (columns,) * 2
        + (P(),) * 2,
        out_specs=(rows,)
        + (grid,) * 4
        + (columns,) * 4
        + (mdl_rows,) * 4
        + (columns,) * 3
        + (P(),) * 3,
        check_vma=False,
    )
```

profile of v0, /device:TPU:0, one launch (start us, length us, event | category | flops | bytes accessed | tf_op | source)
XLA Modules:
  0.0 1000.3 jit_solution(2400045335157976259)
XLA Ops:
  9.8 13.0 %subtract_convert_fusion = (bf16[2048,32]{0,1:T(8,128)(2,1)S(1)}, bf16[2048,32]{0,1:T(8,128)(2,1)S(1)}) fusion(bf16[8192,32]{0,1:T(8,128)(2,1)S(1)} %copy-done, s32[8192]{0:T(1024)S(1)} %fusion.37), kind=kOutput, calls=%fused_computation.68 | convolution fusion | flops 1090846720 | bytes 819200 | tf_op jit(solution)/shard_map/dot_general | solution.py:134
  26.4 18.5 %all_to_all.48 = bf16[8,2,8192]{2,1,0:T(2,128)(2,1)S(1)} all-to-all(bf16[8,2,8192]{2,1,0:T(2,128)(2,1)S(1)} %reshape.107), channel_id=1, replica_groups=mesh['ids'=8,'mdl'=4] {'ids'}, dimensions={0} | all-to-all | bytes 524288 | tf_op jit(solution)/shard_map/all_to_all | solution.py:141
  57.1 5.6 reshape.96
  81.7 48.9 %all_gather.27 = f32[4,2048]{1,0:T(4,128)S(1)} all-gather(f32[4,512]{1,0:T(4,128)S(1)} %pad.17), channel_id=1, replica_groups=mesh['ids'=8,'mdl'=4] {'mdl'}, dimensions={1}, use_global_device_ids=true | all-gather | bytes 40960 | tf_op jit(solution)/shard_map/all_gather | solution.py:118
  130.7 5.4 all_gather.32
  140.1 6.3 fusion.4
  147.0 11.5 %multiply_reduce_fusion.1 = (f32[2048]{0:T(1024)S(1)}, f32[2048]{0:T(1024)S(1)}, f32[1024,2048]{1,0:T(8,128)}) fusion(f32[1024]{0:T(1024)S(1)} %bitcast.109, bf16[1024,1024]{0,1:T(8,128)(2,1)S(1)} %bitcast.85, bf16[1024,2048]{0,1:T(8,128)(2,1)} %all-gather.7.cloned.1.call-done), kind=kOutput, calls=%fused_computation.19 | convolution fusion | flops 4318031872 | bytes 14700544 | tf_op jit(solution)/shard_map/dot_general | solution.py:156
  158.5 39.1 %all-reduce.6 = (f32[2,2048]{1,0:T(2,128)S(1)}, f32[]{:T(128)}) all-reduce(f32[2,2048]{1,0:T(2,128)S(1)} %pad_maximum_fusion.3, f32[]{:T(128)} %get-tuple-element.151), channel_id=1, replica_groups=mesh['ids'=8,'mdl'=4] {'ids','mdl'}, use_global_device_ids=true, to_apply=%region_2.3 | all-reduce | flops 4097 | bytes 32776 | tf_op jit(solution)/shard_map/psum | solution.py:160
  198.9 7.3 add_convert_fusion.1
  206.2 18.3 %multiply_reduce_fusion = (f32[2048]{0:T(1024)S(1)}, f32[2048]{0:T(1024)S(1)}, f32[1024,2048]{1,0:T(8,128)}, f32[1024,2048]{1,0:T(8,128)}) fusion(f32[1024]{0:T(1024)S(1)} %bitcast.110, bf16[1024,2048]{1,0:T(8,128)(2,1)} %add_convert_fusion.1, bf16[2048,2048]{0,1:T(8,128)(2,1)} %all-gather.11.cloned.1.call-done), kind=kOutput, calls=%fused_computation.17 | convolution fusion | flops 8612999168 | bytes 29380608 | tf_op jit(solution)/shard_map/dot_general | solution.py:165
  224.5 40.1 %psum.58 = f32[2,2048]{1,0:T(2,128)S(1)} all-reduce(f32[2,2048]{1,0:T(2,128)S(1)} %pad_maximum_fusion.4), channel_id=1, replica_groups=mesh['ids'=8,'mdl'=4] {'ids','mdl'}, use_global_device_ids=true, to_apply=%region_7.8 | all-reduce | flops 4096 | bytes 32768 | tf_op jit(solution)/shard_map/psum | solution.py:168
  265.5 5.1 convert_reduce_fusion
  274.9 40.2 %psum.59 = f32[2,2048]{1,0:T(2,128)S(1)} all-reduce(f32[2,2048]{1,0:T(2,128)S(1)} %pad_maximum_fusion.5), channel_id=1, replica_groups=mesh['ids'=8,'mdl'=4] {'ids','mdl'}, use_global_device_ids=true, to_apply=%region_10.11 | all-reduce | flops 4096 | bytes 32768 | tf_op jit(solution)/shard_map/psum | solution.py:198
  315.1 12.7 %multiply_convert_fusion.1 = bf16[1024,2048]{1,0:T(8,128)(2,1)S(1)} fusion(f32[1024,2048]{1,0:T(8,128)} %get-tuple-element.167, f32[1024,2048]{1,0:T(8,128)} %get-tuple-element.165, f32[1024,2048]{1,0:T(8,128)} %get-tuple-element.148, f32[]{:T(128)} %get-tuple-element.125, f32[2048]{0:T(1024)S(1)} %bitcast.120, f32[2048]{0:T(1024)S(1)} %bitcast.119, ...), kind=kLoop, calls=%fused_computation.25 | loop fusion | flops 52428800 | bytes 29405188 | tf_op jit(solution)/shard_map/convert_element_type | solution.py:213
  327.8 18.4 %multiply_reduce_fusion.2 = (f32[2048]{0:T(1024)S(1)}, f32[2048]{0:T(1024)S(1)}, f32[1024,2048]{1,0:T(8,128)}) fusion(f32[2048]{0:T(1024)S(1)} %bitcast.94, f32[2048]{0:T(1024)S(1)} %bitcast.97, f32[1024,2048]{1,0:T(8,128)} %get-tuple-element.164, bf16[1024,2048]{1,0:T(8,128)(2,1)S(1)} %multiply_convert_fusion.1, ...), kind=kOutput, calls=%fused_computation.24 | convolution fusion | flops 8615096320 | bytes 29392896 | tf_op jit(solution)/shard_map/dot_general | solution.py:36
  346.2 40.7 %all-reduce.5 = (f32[2,2048]{1,0:T(2,128)S(1)}, f32[32]{0:T(128)S(1)}) all-reduce(f32[2,2048]{1,0:T(2,128)S(1)} %pad_maximum_fusion.6, f32[32]{0:T(128)S(1)} %get-tuple-element.144), channel_id=1, replica_groups=mesh['ids'=8,'mdl'=4] {'ids','mdl'}, use_global_device_ids=true, to_apply=%region_13.14 | all-reduce | flops 4128 | bytes 33024 | tf_op jit(solution)/shard_map/psum | solution.py:224
  386.9 11.3 %multiply_convert_fusion = bf16[1024,2048]{1,0:T(8,128)(2,1)S(1)} fusion(f32[1024,2048]{1,0:T(8,128)} %get-tuple-element.168, f32[1024,2048]{1,0:T(8,128)} %get-tuple-element.164, f32[2048]{0:T(1024)S(1)} %bitcast.114, f32[2048]{0:T(1024)S(1)} %bitcast.113, f32[]{:T(128)} %get-tuple-element.125, f32[2048]{0:T(1024)S(1)} %bitcast.95, f32[2048]{0:T(1024)S(1)} %bitcast.98, ...), kind=kLoop, calls=%fused_computation.23 | loop fusion | flops 54525952 | bytes 21016580 | tf_op jit(solution)/shard_map/convert_element_type | solution.py:242
  419.4 6.5 pad_maximum_fusion
  426.1 5.7 fusion.32
  431.8 47.1 %reduce-scatter.4.cloned.1.call-done = f32[1,1024,512]{2,1,0:T(8,128)} async-done(((f32[4,1024,512]{2,1,0:T(8,128)}), f32[1,1024,512]{2,1,0:T(8,128)}) %reduce-scatter.4.cloned.1.call-update) | async-done | bytes 2097168 | tf_op jit(solution)/shard_map/reduce_scatter | solution.py:249
  479.0 127.4 %reduce-scatter.8.cloned.1.call-done = f32[1,2048,512]{2,1,0:T(8,128)} async-done(((f32[4,2048,512]{2,1,0:T(8,128)}), f32[1,2048,512]{2,1,0:T(8,128)}) %reduce-scatter.8.cloned.1.call-update) | async-done | bytes 4194320 | tf_op jit(solution)/shard_map/reduce_scatter | solution.py:220
  607.7 6.0 all_gather.33
  613.7 6.8 fusion.18
  623.3 5.5 all-to-all-start.3
  630.0 109.6 %all-reduce.12.cloned.1.call-done = f32[2048,32]{0,1:T(8,128)} async-done(((f32[2048,32]{0,1:T(8,128)}), f32[2048,32]{0,1:T(8,128)}) %all-reduce.12.cloned.1.call-update) | async-done | bytes 262160 | tf_op jit(solution)/shard_map/psum | solution.py:224
  742.6 15.7 %all_gather.34 = bf16[8,1024,32]{2,1,0:T(8,128)(2,1)S(1)} all-gather(bf16[8,256,32]{2,1,0:T(8,128)(2,1)S(1)} %reshape.98), channel_id=1, replica_groups=mesh['ids'=8,'mdl'=4] {'mdl'}, dimensions={1}, use_global_device_ids=true | all-gather | bytes 655360 | tf_op jit(solution)/shard_map/all_gather | solution.py:185
  758.3 14.1 %fusion.19 = bf16[2048,32]{0,1:T(8,128)(2,1)S(1)} fusion(bf16[8192,32]{1,0:T(8,128)(2,1)S(1)} %bitcast.83, s32[2048]{0:T(1024)S(1)} %dynamic-slice-done), kind=kOutput, calls=%fused_computation.48 | convolution fusion | flops 1090584576 | bytes 663552 | tf_op jit(solution)/shard_map/dot_general | solution.py:192
  772.4 7.5 all_gather.35
  779.9 30.7 %reduce-scatter.6.cloned.1.call-done = f32[128,512]{1,0:T(8,128)} async-done(((f32[1024,512]{1,0:T(8,128)}), f32[128,512]{1,0:T(8,128)}) %reduce-scatter.6.cloned.1.call-update) | async-done | bytes 262160 | tf_op jit(solution)/shard_map/reduce_scatter | solution.py:250
  815.0 154.8 %all-reduce.10.cloned.1.call-done = f32[4,512,512]{2,1,0:T(8,128)} async-done(((f32[4,512,512]{2,1,0:T(8,128)}), f32[4,512,512]{2,1,0:T(8,128)}) %all-reduce.10.cloned.1.call-update) | async-done | bytes 4194320 | tf_op jit(solution)/shard_map/psum | solution.py:221
  978.3 5.2 copy.103
  983.5 9.0 fusion.48
  (148 shorter events, 90.7 us)
Async XLA Ops:
  7.2 46.1 %all-gather.5.cloned.1.call-start = ((), (), s32[]{:S(2)}) async-start(), calls=%async_computation.7 | async-start | bytes 1179648 | tf_op jit(solution)/shard_map/all_gather | solution.py:109
  9.0 129.6 %all-gather.9.cloned.1.call-start = ((), (), s32[]{:S(2)}) async-start(), calls=%async_computation.9 | async-start | bytes 1310720 | tf_op jit(solution)/shard_map/all_gather | solution.py:142
  48.2 98.8 %all-gather.7.cloned.1.call-start = ((), (), s32[]{:S(2)}) async-start(), calls=%async_computation.8 | async-start | bytes 5242880 | tf_op jit(solution)/shard_map/all_gather | solution.py:110
  53.3 12.3 %copy-start.17 = (s32[8,1024]{1,0:T(8,128)S(1)}, s32[8,1024]{1,0:T(8,128)}, u32[]{:S(2)}) copy-start(s32[8,1024]{1,0:T(8,128)} %param.21) | copy-start | bytes 98308
  53.3 12.3 %copy-start.20 = (s32[8]{0:T(128)S(1)}, s32[8]{0:T(128)}, u32[]{:S(2)}) copy-start(s32[8]{0:T(128)} %param.22) | copy-start | bytes 100
  53.3 152.9 %all-gather.11.cloned.1.call-start = ((), (), s32[]{:S(2)}) async-start(), calls=%async_computation.10 | async-start | bytes 10485760 | tf_op jit(solution)/shard_map/all_gather | solution.py:115
  63.5 18.1 %copy-start.8 = (f32[450,32]{0,1:T(8,128)S(1)}, f32[450,32]{0,1:T(8,128)}, u32[]{:S(2)}) copy-start(f32[450,32]{0,1:T(8,128)} %param.27) | copy-start | bytes 172804
  63.5 18.2 %copy-start.15 = (f32[4,450]{1,0:T(4,128)S(1)}, f32[4,450]{1,0:T(4,128)}, u32[]{:S(2)}) copy-start(f32[4,450]{1,0:T(4,128)} %param.28) | copy-start | bytes 21604
  66.3 11.7 %all-to-all-start = ((s32[8,1,1024]{2,1,0:T(1,128)}), s32[8,1,1024]{2,1,0:T(1,128)S(1)}, u32[]{:S(2)}, u32[]{:S(2)}) async-start(s32[8,1,1024]{2,1,0:T(1,128)} %all_to_all.32), calls=%async_computation | async-start | bytes 65536 | tf_op jit(solution)/shard_map/all_to_all | solution.py:127
  78.0 68.4 %copy-start.12 = (s32[8,1,1024]{2,1,0:T(1,128)}, s32[8,1,1024]{2,1,0:T(1,128)S(1)}, u32[]{:S(2)}) copy-start(s32[8,1,1024]{2,1,0:T(1,128)S(1)} %all-to-all-done) | copy-start | bytes 98308
  78.0 58.2 %all-to-all-start.1 = ((bf16[4,1024,256]{2,1,0:T(8,128)(2,1)}), bf16[4,1024,256]{2,1,0:T(8,128)(2,1)S(1)}, u32[]{:S(2)}, u32[]{:S(2)}) async-start(bf16[4,1024,256]{2,1,0:T(8,128)(2,1)} %bitcast.3), calls=%async_computation.1 | async-start | bytes 4194304 | tf_op jit(solution)/shard_map/all_to_all | solution.py:120
  81.6 397.3 %reduce-scatter.4.cloned.1.call-start = ((), (), s32[]{:S(2)}) async-start(), calls=%async_computation.11 | async-start | bytes 10485760 | tf_op jit(solution)/shard_map/reduce_scatter | solution.py:249
  206.2 59.3 %copy-start.21 = (f32[32]{0:T(128)S(1)}, f32[32]{0:T(128)}, u32[]{:S(2)}) copy-start(f32[32]{0:T(128)} %param.29) | copy-start | bytes 388
  327.8 18.4 %copy-start.4 = (bf16[1024,2048]{1,0:T(8,128)(2,1)}, bf16[1024,2048]{1,0:T(8,128)(2,1)S(1)}, u32[]{:S(2)}) copy-start(bf16[1024,2048]{1,0:T(8,128)(2,1)S(1)} %multiply_convert_fusion.1) | copy-start | bytes 12582916
  406.9 199.5 %reduce-scatter.8.cloned.1.call-start = ((), (), s32[]{:S(2)}) async-start(), calls=%async_computation.13 | async-start | bytes 20971520 | tf_op jit(solution)/shard_map/reduce_scatter | solution.py:220
  426.0 180.5 %copy-start.7 = (f32[128,450]{0,1:T(8,128)S(1)}, f32[128,450]{0,1:T(8,128)}, u32[]{:S(2)}) copy-start(f32[128,450]{0,1:T(8,128)} %param.25) | copy-start | bytes 691204
  426.0 180.7 %copy-start.10 = (f32[128,450]{0,1:T(8,128)S(1)}, f32[128,450]{0,1:T(8,128)}, u32[]{:S(2)}) copy-start(f32[128,450]{0,1:T(8,128)} %param.31) | copy-start | bytes 691204
  426.0 180.8 %copy-start.11 = (f32[128,450]{0,1:T(8,128)S(1)}, f32[128,450]{0,1:T(8,128)}, u32[]{:S(2)}) copy-start(f32[128,450]{0,1:T(8,128)} %param.30) | copy-start | bytes 691204
  426.0 313.6 %all-reduce.12.cloned.1.call-start = ((), (), s32[]{:S(2)}) async-start(), calls=%async_computation.15 | async-start | bytes 524288 | tf_op jit(solution)/shard_map/psum | solution.py:224
  431.8 378.8 %reduce-scatter.6.cloned.1.call-start = ((), (), s32[]{:S(2)}) async-start(), calls=%async_computation.12 | async-start | bytes 2359296 | tf_op jit(solution)/shard_map/reduce_scatter | solution.py:250
  478.9 490.8 %all-reduce.10.cloned.1.call-start = ((), (), s32[]{:S(2)}) async-start(), calls=%async_computation.14 | async-start | bytes 8388608 | tf_op jit(solution)/shard_map/psum | solution.py:221
  606.6 22.2 %copy-start.22 = (f32[32]{0:T(128)S(1)}, f32[32]{0:T(128)}, u32[]{:S(2)}) copy-start(f32[32]{0:T(128)} %param.39) | copy-start | bytes 388
  606.6 22.2 %copy-start.23 = (f32[32]{0:T(128)S(1)}, f32[32]{0:T(128)}, u32[]{:S(2)}) copy-start(f32[32]{0:T(128)} %param.38) | copy-start | bytes 388
  606.6 22.7 %copy-start.16 = (f32[4,450]{1,0:T(4,128)S(1)}, f32[4,450]{1,0:T(4,128)}, u32[]{:S(2)}) copy-start(f32[4,450]{1,0:T(4,128)} %param.28) | copy-start | bytes 21604
  606.6 22.7 %copy-start.18 = (f32[4,450]{1,0:T(4,128)S(1)}, f32[4,450]{1,0:T(4,128)}, u32[]{:S(2)}) copy-start(f32[4,450]{1,0:T(4,128)} %param.37) | copy-start | bytes 21604
  606.6 22.7 %copy-start.19 = (f32[4,450]{1,0:T(4,128)S(1)}, f32[4,450]{1,0:T(4,128)}, u32[]{:S(2)}) copy-start(f32[4,450]{1,0:T(4,128)} %param.36) | copy-start | bytes 21604
  606.7 133.0 %copy-start.9 = (f32[450,32]{0,1:T(8,128)S(1)}, f32[450,32]{0,1:T(8,128)}, u32[]{:S(2)}) copy-start(f32[450,32]{0,1:T(8,128)} %param.27) | copy-start | bytes 172804
  606.7 133.0 %copy-start.13 = (f32[450,32]{0,1:T(8,128)S(1)}, f32[450,32]{0,1:T(8,128)}, u32[]{:S(2)}) copy-start(f32[450,32]{0,1:T(8,128)} %param.35) | copy-start | bytes 172804
  606.7 133.0 %copy-start.14 = (f32[450,32]{0,1:T(8,128)S(1)}, f32[450,32]{0,1:T(8,128)}, u32[]{:S(2)}) copy-start(f32[450,32]{0,1:T(8,128)} %param.34) | copy-start | bytes 172804
  613.7 144.6 %dynamic-slice-start = ((s32[8192]{0:T(1024)}, s32[]{:T(128)}), s32[2048]{0:T(1024)S(1)}, s32[]{:S(2)}) async-start(s32[8192]{0:T(1024)} %param.23, s32[]{:T(128)} %select_n.30), calls=%async_computation.16 | async-start | bytes 16896 | tf_op jit(solution)/shard_map/dynamic_slice | solution.py:187
  623.3 118.1 %all-to-all-start.3 = ((bf16[8,2,4096]{2,1,0:T(2,128)(2,1)}), bf16[8,2,4096]{2,1,0:T(2,128)(2,1)S(1)}, u32[]{:S(2)}, u32[]{:S(2)}) async-start(bf16[8,2,4096]{2,1,0:T(2,128)(2,1)} %reshape.109), calls=%async_computation.3 | async-start | bytes 262144 | tf_op jit(solution)/shard_map/all_to_all | solution.py:184
  978.3 14.9 %copy-start.1 = (bf16[8192,32]{0,1:T(8,128)(2,1)S(1)}, bf16[8192,32]{0,1:T(8,128)(2,1)}, u32[]{:S(2)}) copy-start(bf16[8192,32]{0,1:T(8,128)(2,1)} %param.24) | copy-start | bytes 1572868
  (5 other events, 25.7 us)
Sparse Core Ops, SparseCore 0:
  10.6 42.5 all-gather.4
  55.4 17.2 all-gather.8
  74.3 56.9 all-gather.6
  133.3 57.1 all-gather.10
  407.0 71.8 reduce-scatter.3
  481.3 125.0 reduce-scatter.7
  612.5 127.0 all-reduce.11
  743.2 67.4 reduce-scatter.5
  814.3 155.4 all-reduce.9
where the time goes:
time: 1010 us; the launch traced here: 1000 us
  waiting for transfers between devices  477 us (47%)
  blocking collectives  262 us (26%)
  matrix products  121 us (12%)
  other arithmetic  72.2 us (7%)
  local copies, waits for them, and re-layouts  37.4 us (4%)
  between operations  15.7 us (2%)
  starting transfers between devices  15 us (1%)
    psum x1, waiting for transfers between devices, body(): grad_second = lax.psum(grad_second, 'ids')  155 us
    reduce_scatter x1, waiting for transfers between devices, body(): lax.psum_scatter(local_second, 'mdl', scatter_dimension=0, tiled=False)  127 us
    psum x1, waiting for transfers between devices, body(): lax.psum((jnp.stack([jnp.sum(incoming_one * unit_one, 0), jnp.sum(incomin...  110 us
    all_gather x1, blocking collectives, body(): lax.all_gather(jnp.pad(norm_params, ((0, 0), (0, more))), 'mdl', axis=1,...  48.9 us
    reduce_scatter x1, waiting for transfers between devices, body(): lax.psum_scatter(local_first, 'mdl', scatter_dimension=0, tiled=False)  47.1 us
    dot_general x11, matrix products, contract(): lax.dot_general(left, right, (((left_dim,), (right_dim,)), ((), ())), pre...  45.5 us
    psum x1, blocking collectives, body(): lax.psum((jnp.stack([jnp.sum(incoming_one * unit_one, 0), jnp.sum(incomin...  40.7 us
    psum x1, blocking collectives, body(): lax.psum(jnp.stack([jnp.sum(incoming_two * unit_two, 0), jnp.sum(incoming...  40.2 us
  transfers between devices with their start and end apart: 12, of which 7 were waited for; matrix products, arithmetic and copies ran while one was open for 12% of the time, Pallas kernels for 0%

commit v1 on v0

--- a/solution.py
+++ b/solution.py
@@ -14,6 +14,12 @@
 rate_norm = 0.5
 rate_bias = 0.02
 LANES = 128
+
+
+def plan_tracks(block_here, axis_id):
+    o_now = lax.all_gather(block_here, axis_id)
+    part_now = jnp.sum(o_now, axis=0)
+    return part_now
 
 
 def mish_parts(inputs):
@@ -218,7 +224,7 @@
         ]
     )
     grad_second = lax.psum_scatter(local_second, "mdl", scatter_dimension=0, tiled=False)
-    grad_second = lax.psum(grad_second, "ids")
+    grad_second = plan_tracks(grad_second, "ids")
     grad_second = grad_second.reshape(parts, wide, wide)[:, :width, :width].reshape(-1, width)
     incoming_one = contract(grad_linear_two, second_low, 1, 1)
     sums_one, final_sum, grad_bias = lax.psum(

time: 1010 us -> 1500 us (1.49)
  waiting for transfers between devices: 477 us -> 956 us
  other arithmetic: 72.2 us -> 87.3 us
    all_gather x0 -> x1, waiting for transfers between devices: none -> 634 us  [plan_tracks(): o_now = lax.all_gather(block_here, axis_id)]
    psum x1 -> x0, waiting for transfers between devices: 155 us -> none  [body(): grad_second = lax.psum(grad_second, 'ids')]
    reduce_sum x0 -> x1, other arithmetic: none -> 15.1 us  [plan_tracks(): part_now = jnp.sum(o_now, axis=0)]
  transfers between devices with their start and end apart: 12 -> 12, of which waited for: 7 -> 7; matrix products, arithmetic and copies ran while one was open for 12% -> 8% of each run, Pallas kernels for 0% -> 0%
where the time goes in v1:
time: 1500 us; the launch traced here: 1490 us
  waiting for transfers between devices  956 us (64%)
  blocking collectives  262 us (17%)
  matrix products  121 us (8%)
  other arithmetic  87.3 us (6%)
  local copies, waits for them, and re-layouts  37.5 us (2%)
  between operations  15.7 us (1%)
  starting transfers between devices  15 us (1%)
    all_gather x1, waiting for transfers between devices, plan_tracks(): o_now = lax.all_gather(block_here, axis_id)  634 us
    reduce_scatter x1, waiting for transfers between devices, body(): lax.psum_scatter(local_second, 'mdl', scatter_dimension=0, tiled=False)  127 us
    psum x1, waiting for transfers between devices, body(): lax.psum((jnp.stack([jnp.sum(incoming_one * unit_one, 0), jnp.sum(incomin...  110 us
    all_gather x1, blocking collectives, body(): lax.all_gather(jnp.pad(norm_params, ((0, 0), (0, more))), 'mdl', axis=1,...  48.9 us
    reduce_scatter x1, waiting for transfers between devices, body(): lax.psum_scatter(local_first, 'mdl', scatter_dimension=0, tiled=False)  47.1 us
    dot_general x11, matrix products, contract(): lax.dot_general(left, right, (((left_dim,), (right_dim,)), ((), ())), pre...  45.5 us
    psum x1, blocking collectives, body(): lax.psum((jnp.stack([jnp.sum(incoming_one * unit_one, 0), jnp.sum(incomin...  40.7 us
    psum x1, blocking collectives, body(): lax.psum(jnp.stack([jnp.sum(incoming_two * unit_two, 0), jnp.sum(incoming...  40.2 us
  transfers between devices with their start and end apart: 12, of which 7 were waited for; matrix products, arithmetic and copies ran while one was open for 8% of the time, Pallas kernels for 0%

profile of v1, /device:TPU:0, one launch (start us, length us, event | category | flops | bytes accessed | tf_op | source)
XLA Modules:
  0.0 1494.5 jit_solution(9010512587461533780)
XLA Ops:
  9.8 13.0 subtract_convert_fusion
  26.4 18.5 %all_to_all.48 = bf16[8,2,8192]{2,1,0:T(2,128)(2,1)S(1)} all-to-all(bf16[8,2,8192]{2,1,0:T(2,128)(2,1)S(1)} %reshape.106), channel_id=1, replica_groups=mesh['ids'=8,'mdl'=4] {'ids'}, dimensions={0} | all-to-all | bytes 524288 | tf_op jit(solution)/shard_map/all_to_all | solution.py:147
  57.1 5.6 reshape.96
  81.7 48.9 %all_gather.30 = f32[4,2048]{1,0:T(4,128)S(1)} all-gather(f32[4,512]{1,0:T(4,128)S(1)} %pad.17), channel_id=1, replica_groups=mesh['ids'=8,'mdl'=4] {'mdl'}, dimensions={1}, use_global_device_ids=true | all-gather | bytes 40960 | tf_op jit(solution)/shard_map/all_gather | solution.py:124
  130.7 5.4 all_gather.35
  140.1 6.3 fusion.4
  147.0 11.5 multiply_reduce_fusion.1
  158.5 39.1 %all-reduce.6 = (f32[2,2048]{1,0:T(2,128)S(1)}, f32[]{:T(128)}) all-reduce(f32[2,2048]{1,0:T(2,128)S(1)} %pad_maximum_fusion.3, f32[]{:T(128)} %get-tuple-element.151), channel_id=1, replica_groups=mesh['ids'=8,'mdl'=4] {'ids','mdl'}, use_global_device_ids=true, to_apply=%region_2.3 | all-reduce | flops 4097 | bytes 32776 | tf_op jit(solution)/shard_map/psum | solution.py:166
  198.9 7.3 add_convert_fusion.1
  206.2 18.3 %multiply_reduce_fusion = (f32[2048]{0:T(1024)S(1)}, f32[2048]{0:T(1024)S(1)}, f32[1024,2048]{1,0:T(8,128)}, f32[1024,2048]{1,0:T(8,128)}) fusion(f32[1024]{0:T(1024)S(1)} %bitcast.110, bf16[1024,2048]{1,0:T(8,128)(2,1)} %add_convert_fusion.1, bf16[2048,2048]{0,1:T(8,128)(2,1)} %all-gather.12.cloned.1.call-done), kind=kOutput, calls=%fused_computation.17 | convolution fusion | flops 8612999168 | bytes 29380608 | tf_op jit(solution)/shard_map/dot_general | solution.py:171
  224.5 40.1 %psum.51 = f32[2,2048]{1,0:T(2,128)S(1)} all-reduce(f32[2,2048]{1,0:T(2,128)S(1)} %pad_maximum_fusion.4), channel_id=1, replica_groups=mesh['ids'=8,'mdl'=4] {'ids','mdl'}, use_global_device_ids=true, to_apply=%region_7.8 | all-reduce | flops 4096 | bytes 32768 | tf_op jit(solution)/shard_map/psum | solution.py:174
  274.9 40.2 %psum.52 = f32[2,2048]{1,0:T(2,128)S(1)} all-reduce(f32[2,2048]{1,0:T(2,128)S(1)} %pad_maximum_fusion.5), channel_id=1, replica_groups=mesh['ids'=8,'mdl'=4] {'ids','mdl'}, use_global_device_ids=true, to_apply=%region_10.11 | all-reduce | flops 4096 | bytes 32768 | tf_op jit(solution)/shard_map/psum | solution.py:204
  315.1 12.7 multiply_convert_fusion.1
  327.8 18.4 %multiply_reduce_fusion.2 = (f32[2048]{0:T(1024)S(1)}, f32[2048]{0:T(1024)S(1)}, f32[1024,2048]{1,0:T(8,128)}) fusion(f32[2048]{0:T(1024)S(1)} %bitcast.94, f32[2048]{0:T(1024)S(1)} %bitcast.97, f32[1024,2048]{1,0:T(8,128)} %get-tuple-element.164, bf16[1024,2048]{1,0:T(8,128)(2,1)S(1)} %multiply_convert_fusion.1, ...), kind=kOutput, calls=%fused_computation.24 | convolution fusion | flops 8615096320 | bytes 29392896 | tf_op jit(solution)/shard_map/dot_general | solution.py:42
  346.2 40.7 %all-reduce.5 = (f32[2,2048]{1,0:T(2,128)S(1)}, f32[32]{0:T(128)S(1)}) all-reduce(f32[2,2048]{1,0:T(2,128)S(1)} %pad_maximum_fusion.6, f32[32]{0:T(128)S(1)} %get-tuple-element.144), channel_id=1, replica_groups=mesh['ids'=8,'mdl'=4] {'ids','mdl'}, use_global_device_ids=true, to_apply=%region_13.14 | all-reduce | flops 4128 | bytes 33024 | tf_op jit(solution)/shard_map/psum | solution.py:230
  386.9 11.3 multiply_convert_fusion
  419.4 6.5 pad_maximum_fusion
  426.1 5.7 fusion.32
  431.8 47.1 %reduce-scatter.4.cloned.1.call-done = f32[1,1024,512]{2,1,0:T(8,128)} async-done(((f32[4,1024,512]{2,1,0:T(8,128)}), f32[1,1024,512]{2,1,0:T(8,128)}) %reduce-scatter.4.cloned.1.call-update) | async-done | bytes 2097168 | tf_op jit(solution)/shard_map/reduce_scatter | solution.py:255
  479.0 127.4 %reduce-scatter.8.cloned.1.call-done = f32[1,2048,512]{2,1,0:T(8,128)} async-done(((f32[4,2048,512]{2,1,0:T(8,128)}), f32[1,2048,512]{2,1,0:T(8,128)}) %reduce-scatter.8.cloned.1.call-update) | async-done | bytes 4194320 | tf_op jit(solution)/shard_map/reduce_scatter | solution.py:226
  607.7 6.0 all_gather.36
  613.7 6.8 fusion.18
  623.3 5.5 all-to-all-start.3
  630.0 109.6 %all-reduce.9.cloned.1.call-done = f32[2048,32]{0,1:T(8,128)} async-done(((f32[2048,32]{0,1:T(8,128)}), f32[2048,32]{0,1:T(8,128)}) %all-reduce.9.cloned.1.call-update) | async-done | bytes 262160 | tf_op jit(solution)/shard_map/psum | solution.py:230
  742.6 15.7 %all_gather.37 = bf16[8,1024,32]{2,1,0:T(8,128)(2,1)S(1)} all-gather(bf16[8,256,32]{2,1,0:T(8,128)(2,1)S(1)} %reshape.98), channel_id=1, replica_groups=mesh['ids'=8,'mdl'=4] {'mdl'}, dimensions={1}, use_global_device_ids=true | all-gather | bytes 655360 | tf_op jit(solution)/shard_map/all_gather | solution.py:191
  758.3 14.1 fusion.19
  772.4 7.5 all_gather.38
  779.9 30.7 %reduce-scatter.6.cloned.1.call-done = f32[128,512]{1,0:T(8,128)} async-done(((f32[1024,512]{1,0:T(8,128)}), f32[128,512]{1,0:T(8,128)}) %reduce-scatter.6.cloned.1.call-update) | async-done | bytes 262160 | tf_op jit(solution)/shard_map/reduce_scatter | solution.py:256
  815.0 633.9 %all-gather.14.cloned.1.call-done = f32[8,2048,512]{2,1,0:T(8,128)} async-done(((f32[1,2048,512]{2,1,0:T(8,128)}), f32[8,2048,512]{2,1,0:T(8,128)}) %all-gather.14.cloned.1.call-update) | async-done | bytes 33554448 | tf_op jit(solution)/shard_map/all_gather | solution.py:20
  1448.9 15.1 %reduce_sum.108 = f32[2048,512]{1,0:T(8,128)} reduce(f32[8,2048,512]{2,1,0:T(8,128)} %all-gather.14.cloned.1.call-done, f32[]{:T(128)} %constant.41.clone.1), dimensions={0}, to_apply=%region_17.18 | reduce | flops 7340032 | bytes 37748740 | tf_op jit(solution)/shard_map/reduce_sum | solution.py:21
  1472.6 5.2 copy.100
  1477.8 9.0 fusion.48
  (149 shorter events, 95.9 us)
Async XLA Ops:
  7.2 46.1 %all-gather.6.cloned.1.call-start = ((), (), s32[]{:S(2)}) async-start(), calls=%async_computation.7 | async-start | bytes 1179648 | tf_op jit(solution)/shard_map/all_gather | solution.py:115
  9.0 129.6 %all-gather.10.cloned.1.call-start = ((), (), s32[]{:S(2)}) async-start(), calls=%async_computation.9 | async-start | bytes 1310720 | tf_op jit(solution)/shard_map/all_gather | solution.py:148
  48.2 98.8 %all-gather.8.cloned.1.call-start = ((), (), s32[]{:S(2)}) async-start(), calls=%async_computation.8 | async-start | bytes 5242880 | tf_op jit(solution)/shard_map/all_gather | solution.py:116
  53.3 12.3 copy-start.17
  53.3 12.3 copy-start.20
  53.3 152.9 %all-gather.12.cloned.1.call-start = ((), (), s32[]{:S(2)}) async-start(), calls=%async_computation.10 | async-start | bytes 10485760 | tf_op jit(solution)/shard_map/all_gather | solution.py:121
  63.5 18.1 %copy-start.8 = (f32[450,32]{0,1:T(8,128)S(1)}, f32[450,32]{0,1:T(8,128)}, u32[]{:S(2)}) copy-start(f32[450,32]{0,1:T(8,128)} %param.27) | copy-start | bytes 172804
  63.5 18.2 %copy-start.15 = (f32[4,450]{1,0:T(4,128)S(1)}, f32[4,450]{1,0:T(4,128)}, u32[]{:S(2)}) copy-start(f32[4,450]{1,0:T(4,128)} %param.28) | copy-start | bytes 21604
  66.3 11.7 all-to-all-start
  78.0 68.4 %copy-start.12 = (s32[8,1,1024]{2,1,0:T(1,128)}, s32[8,1,1024]{2,1,0:T(1,128)S(1)}, u32[]{:S(2)}) copy-start(s32[8,1,1024]{2,1,0:T(1,128)S(1)} %all-to-all-done) | copy-start | bytes 98308
  78.0 58.2 %all-to-all-start.1 = ((bf16[4,1024,256]{2,1,0:T(8,128)(2,1)}), bf16[4,1024,256]{2,1,0:T(8,128)(2,1)S(1)}, u32[]{:S(2)}, u32[]{:S(2)}) async-start(bf16[4,1024,256]{2,1,0:T(8,128)(2,1)} %bitcast.3), calls=%async_computation.1 | async-start | bytes 4194304 | tf_op jit(solution)/shard_map/all_to_all | solution.py:126
  81.6 397.3 %reduce-scatter.4.cloned.1.call-start = ((), (), s32[]{:S(2)}) async-start(), calls=%async_computation.11 | async-start | bytes 10485760 | tf_op jit(solution)/shard_map/reduce_scatter | solution.py:255
  206.2 59.3 %copy-start.21 = (f32[32]{0:T(128)S(1)}, f32[32]{0:T(128)}, u32[]{:S(2)}) copy-start(f32[32]{0:T(128)} %param.29) | copy-start | bytes 388
  327.8 18.4 %copy-start.4 = (bf16[1024,2048]{1,0:T(8,128)(2,1)}, bf16[1024,2048]{1,0:T(8,128)(2,1)S(1)}, u32[]{:S(2)}) copy-start(bf16[1024,2048]{1,0:T(8,128)(2,1)S(1)} %multiply_convert_fusion.1) | copy-start | bytes 12582916
  406.9 199.5 %reduce-scatter.8.cloned.1.call-start = ((), (), s32[]{:S(2)}) async-start(), calls=%async_computation.13 | async-start | bytes 20971520 | tf_op jit(solution)/shard_map/reduce_scatter | solution.py:226
  426.0 180.5 %copy-start.7 = (f32[128,450]{0,1:T(8,128)S(1)}, f32[128,450]{0,1:T(8,128)}, u32[]{:S(2)}) copy-start(f32[128,450]{0,1:T(8,128)} %param.25) | copy-start | bytes 691204
  426.0 180.7 %copy-start.10 = (f32[128,450]{0,1:T(8,128)S(1)}, f32[128,450]{0,1:T(8,128)}, u32[]{:S(2)}) copy-start(f32[128,450]{0,1:T(8,128)} %param.31) | copy-start | bytes 691204
  426.0 180.8 %copy-start.11 = (f32[128,450]{0,1:T(8,128)S(1)}, f32[128,450]{0,1:T(8,128)}, u32[]{:S(2)}) copy-start(f32[128,450]{0,1:T(8,128)} %param.30) | copy-start | bytes 691204
  426.0 313.6 %all-reduce.9.cloned.1.call-start = ((), (), s32[]{:S(2)}) async-start(), calls=%async_computation.15 | async-start | bytes 524288 | tf_op jit(solution)/shard_map/psum | solution.py:230
  431.8 378.8 %reduce-scatter.6.cloned.1.call-start = ((), (), s32[]{:S(2)}) async-start(), calls=%async_computation.12 | async-start | bytes 2359296 | tf_op jit(solution)/shard_map/reduce_scatter | solution.py:256
  478.9 970.0 %all-gather.14.cloned.1.call-start = ((), (), s32[]{:S(2)}) async-start(), calls=%async_computation.14 | async-start | bytes 37748736 | tf_op jit(solution)/shard_map/all_gather | solution.py:20
  606.6 22.2 %copy-start.22 = (f32[32]{0:T(128)S(1)}, f32[32]{0:T(128)}, u32[]{:S(2)}) copy-start(f32[32]{0:T(128)} %param.39) | copy-start | bytes 388
  606.6 22.2 %copy-start.23 = (f32[32]{0:T(128)S(1)}, f32[32]{0:T(128)}, u32[]{:S(2)}) copy-start(f32[32]{0:T(128)} %param.38) | copy-start | bytes 388
  606.6 22.7 %copy-start.16 = (f32[4,450]{1,0:T(4,128)S(1)}, f32[4,450]{1,0:T(4,128)}, u32[]{:S(2)}) copy-start(f32[4,450]{1,0:T(4,128)} %param.28) | copy-start | bytes 21604
  606.6 22.7 %copy-start.18 = (f32[4,450]{1,0:T(4,128)S(1)}, f32[4,450]{1,0:T(4,128)}, u32[]{:S(2)}) copy-start(f32[4,450]{1,0:T(4,128)} %param.37) | copy-start | bytes 21604
  606.6 22.7 %copy-start.19 = (f32[4,450]{1,0:T(4,128)S(1)}, f32[4,450]{1,0:T(4,128)}, u32[]{:S(2)}) copy-start(f32[4,450]{1,0:T(4,128)} %param.36) | copy-start | bytes 21604
  606.7 133.0 %copy-start.9 = (f32[450,32]{0,1:T(8,128)S(1)}, f32[450,32]{0,1:T(8,128)}, u32[]{:S(2)}) copy-start(f32[450,32]{0,1:T(8,128)} %param.27) | copy-start | bytes 172804
  606.7 133.0 %copy-start.13 = (f32[450,32]{0,1:T(8,128)S(1)}, f32[450,32]{0,1:T(8,128)}, u32[]{:S(2)}) copy-start(f32[450,32]{0,1:T(8,128)} %param.35) | copy-start | bytes 172804
  606.7 133.0 %copy-start.14 = (f32[450,32]{0,1:T(8,128)S(1)}, f32[450,32]{0,1:T(8,128)}, u32[]{:S(2)}) copy-start(f32[450,32]{0,1:T(8,128)} %param.34) | copy-start | bytes 172804
  613.7 144.6 %dynamic-slice-start = ((s32[8192]{0:T(1024)}, s32[]{:T(128)}), s32[2048]{0:T(1024)S(1)}, s32[]{:S(2)}) async-start(s32[8192]{0:T(1024)} %param.23, s32[]{:T(128)} %select_n.30), calls=%async_computation.16 | async-start | bytes 16896 | tf_op jit(solution)/shard_map/dynamic_slice | solution.py:193
  623.3 118.1 %all-to-all-start.3 = ((bf16[8,2,4096]{2,1,0:T(2,128)(2,1)}), bf16[8,2,4096]{2,1,0:T(2,128)(2,1)S(1)}, u32[]{:S(2)}, u32[]{:S(2)}) async-start(bf16[8,2,4096]{2,1,0:T(2,128)(2,1)} %reshape.108), calls=%async_computation.3 | async-start | bytes 262144 | tf_op jit(solution)/shard_map/all_to_all | solution.py:190
  1472.6 14.9 %copy-start.1 = (bf16[8192,32]{0,1:T(8,128)(2,1)S(1)}, bf16[8192,32]{0,1:T(8,128)(2,1)}, u32[]{:S(2)}) copy-start(bf16[8192,32]{0,1:T(8,128)(2,1)} %param.24) | copy-start | bytes 1572868
  (5 other events, 25.7 us)
Sparse Core Ops, SparseCore 0:
  10.6 42.5 all-gather.5
  55.4 17.2 all-gather.9
  74.3 56.9 all-gather.7
  133.3 57.1 all-gather.11
  407.0 71.8 reduce-scatter.3
  481.3 125.0 reduce-scatter.7
  612.5 127.0 all-reduce.8
  743.2 67.4 reduce-scatter.5
  812.2 636.6 all-gather.13
